TPU v7x, 32 devices: a whole 2x2x4 slice. The times are simulated.
32 devices in a mesh: rep: 8 (over y, x, core), tp: 4 (over z).
Axes of the slice: x: 2, y: 2, z: 4, core: 2. Of those that a mesh axis runs over, the one named last changes fastest.
Arguments:
- tokens: bfloat16 [4096, 8192], P('rep', 'tp'), may hold values from -6 to 6
- query_weight: bfloat16 [8192, 4096], P(None, 'tp'), may hold values from -0.0625 to 0.0625
- key_value_weight: bfloat16 [8192, 1024], P('tp'), may hold values from -0.0625 to 0.0625
- adapter_down_tables: bfloat16 [32, 192, 8192], P('rep', None, 'tp'), may hold values from -0.0625 to 0.0625
- adapter_up_query: bfloat16 [32, 64, 4096], P('rep', None, 'tp'), may hold values from -0.75 to 0.75
- adapter_up_key_value: bfloat16 [32, 64, 1024], P('rep', None, 'tp'), may hold values from -0.75 to 0.75
- request_adapter: int32 [128], P('rep'), may hold values from 0 to 31, as said below
- request_token_length: int32 [128], P('rep'), may hold values from 8 to 32, as said below
- adapter_table_row: int32 [32], replicated, may hold values from 0 to 31, as said below
Outputs:
- attended: bfloat16 [4096, 4096], P('rep', 'tp')
Inputs may be any that keep to these rules, and one draw needn't show every extreme that they name: `request_adapter`: in each replica's block of 16 requests at most 4 have adapters whose table rows adapter_table_row lies in one index of rep's share (rows s with the same s // 4); in every draw one share gets exactly 4 from every replica. `adapter_table_row`: A permutation of the table rows. `request_token_length`: every replica has one request of exactly 32 tokens.
All inputs are finite; a program needn't handle non-finite values.
Results may differ from a plain program's by a relative error of at most 0.0098.
Values may be sent and summed in bfloat16 or wider, within the bound.
A program may use at most 192 MiB of HBM per device.

v0:
```python
import math
import jax
import jax.numpy as jnp
from jax import lax
from jax.sharding import PartitionSpec as P

HEAD_SIZE = 128
adapter_scale = 0.5
rope_theta = 500000.0


def rotary(values, positions):
    half_dim = values.shape[-1] // 2
    frequency = rope_theta ** (-(jnp.arange(half_dim, dtype=jnp.float32) * 2.0 / values.shape[-1]))
    angles = positions.astype(jnp.float32)[:, None] * frequency[None, :]
    cosine = jnp.cos(angles)[:, None, :]
    sine_part = jnp.sin(angles)[:, None, :]
    lower_half = values[..., :half_dim]
    upper_half = values[..., half_dim:]
    return jnp.concatenate(
        [
            lower_half * cosine - upper_half * sine_part,
            upper_half * cosine + lower_half * sine_part,
        ],
        axis=-1,
    )


def expand_slots(shrink, query_up_weight, key_value_up_weight, value_side):
    rank_size = query_up_weight.shape[2]
    query_change = jnp.einsum(
        "sinr,sirc->sinc",
        shrink[..., :rank_size],
        query_up_weight,
        preferred_element_type=jnp.float32,
    )
    pair_input = jnp.where(
        value_side, shrink[..., 2 * rank_size :], shrink[..., rank_size : 2 * rank_size]
    )
    key_value_update = jnp.einsum(
        "sinr,sirc->sinc", pair_input, key_value_up_weight, preferred_element_type=jnp.float32
    )
    return (adapter_scale * jnp.concatenate([query_change, key_value_update], axis=-1)).astype(
        jnp.bfloat16
    )


def shards(
    tokens,
    query_weight,
    key_value_weight,
    adapter_down_tables,
    adapter_up_query,
    adapter_up_key_value,
    request_adapter,
    request_token_length,
    adapter_table_row,
):
    replicas = lax.axis_size("rep")
    tp_count = lax.axis_size("tp")
    tp_here = lax.axis_index("tp")
    tok_rows = tokens.shape[0]
    feat_local = tokens.shape[1]
    query_cols = query_weight.shape[1]
    pair_total = key_value_weight.shape[1]
    portion_value = adapter_up_key_value.shape[2]
    local_table_rows = adapter_down_tables.shape[0]
    requests_here = request_adapter.shape[0]
    seq_len = tok_rows // requests_here
    capacity = max(1, 2 * requests_here // replicas)
    slot_count = replicas * capacity
    delta_cols = query_cols + portion_value
    value_side = tp_here >= tp_count // 2
    base_query = jnp.dot(
        lax.all_gather(tokens, "tp", axis=1, tiled=True),
        query_weight,
        preferred_element_type=jnp.float32,
    )
    base_pair = jnp.dot(tokens, key_value_weight, preferred_element_type=jnp.float32)
    id_match = (
        request_adapter[:, None] == jnp.arange(adapter_table_row.shape[0], dtype=jnp.int32)[None, :]
    )
    homes = jnp.sum(jnp.where(id_match, adapter_table_row[None, :], 0), axis=1)
    owners = homes // local_table_rows
    local_ids = homes % local_table_rows
    request_pos = jnp.arange(requests_here, dtype=jnp.int32)
    earlier = (owners[:, None] == owners[None, :]) & (request_pos[None, :] < request_pos[:, None])
    slot_ids = owners * capacity + jnp.sum(earlier.astype(jnp.int32), axis=1)
    placement = slot_ids[None, :] == jnp.arange(slot_count, dtype=jnp.int32)[:, None]
    place_matrix = placement.astype(jnp.bfloat16)
    send_rows = jnp.dot(
        place_matrix,
        tokens.reshape(requests_here, seq_len * feat_local),
        preferred_element_type=jnp.float32,
    )
    send_rows = send_rows.astype(jnp.bfloat16).reshape(replicas, capacity, seq_len, feat_local)
    slot_local = jnp.sum(jnp.where(placement, local_ids[None, :], 0), axis=1).reshape(
        replicas, capacity
    )
    needed_locally = lax.all_to_all(slot_local, "rep", split_axis=0, concat_axis=0, tiled=True)
    fetched_down, fetched_query, fetched_pair = (
        lax.all_to_all(
            jnp.take(adapter_down_tables, needed_locally, axis=0),
            "rep",
            split_axis=0,
            concat_axis=0,
            tiled=True,
        ),
        lax.all_to_all(
            jnp.take(adapter_up_query, needed_locally, axis=0),
            "rep",
            split_axis=0,
            concat_axis=0,
            tiled=True,
        ),
        lax.all_to_all(
            jnp.take(adapter_up_key_value, needed_locally, axis=0),
            "rep",
            split_axis=0,
            concat_axis=0,
            tiled=True,
        ),
    )
    partial_sum = jnp.einsum(
        "scnf,scrf->scnr", send_rows, fetched_down, preferred_element_type=jnp.float32
    )
    shrink = lax.psum(partial_sum, "tp").astype(jnp.bfloat16)
    returned = expand_slots(shrink, fetched_query, fetched_pair, value_side)
    delta = jnp.dot(
        place_matrix.T,
        returned.reshape(slot_count, seq_len * delta_cols),
        preferred_element_type=jnp.float32,
    )
    delta = delta.reshape(tok_rows, delta_cols)
    positions = jnp.arange(tok_rows, dtype=jnp.int32) % seq_len
    heads_here = query_cols // HEAD_SIZE
    query = rotary(
        (base_query + delta[:, :query_cols]).reshape(tok_rows, heads_here, HEAD_SIZE), positions
    ).astype(jnp.bfloat16)
    placed = lax.dynamic_update_slice_in_dim(
        jnp.zeros((tok_rows, pair_total), jnp.float32),
        delta[:, query_cols:],
        tp_here * portion_value,
        1,
    )
    pair_full = lax.psum(base_pair + placed, "tp")
    pair_raw = lax.optimization_barrier(pair_full.astype(jnp.bfloat16))
    kv_heads = pair_total // (2 * HEAD_SIZE)
    head_index = tp_here // (tp_count // kv_heads)
    keys_raw = lax.dynamic_slice_in_dim(pair_raw, head_index * HEAD_SIZE, HEAD_SIZE, 1)
    values = lax.dynamic_slice_in_dim(
        pair_raw, kv_heads * HEAD_SIZE + head_index * HEAD_SIZE, HEAD_SIZE, 1
    )
    keys = rotary(keys_raw.astype(jnp.float32).reshape(tok_rows, 1, HEAD_SIZE), positions).astype(
        jnp.bfloat16
    )
    query_blocks = query.reshape(requests_here, seq_len, heads_here, HEAD_SIZE)
    key_blocks = keys.reshape(requests_here, seq_len, HEAD_SIZE)
    value_blocks = values.reshape(requests_here, seq_len, HEAD_SIZE)
    scores = jnp.einsum(
        "rqhd,rpd->rhqp", query_blocks, key_blocks, preferred_element_type=jnp.float32
    ) / math.sqrt(HEAD_SIZE)
    slot_pos = jnp.arange(seq_len, dtype=jnp.int32)
    allowed = (slot_pos[None, None, :] <= slot_pos[None, :, None]) & (
        slot_pos[None, None, :] < request_token_length[:, None, None]
    )
    scores = jnp.where(allowed[:, None, :, :], scores, jnp.float32(-1e30))
    peak = jnp.max(scores, axis=-1, keepdims=True)
    weights = jnp.exp(scores - peak)
    probs = (weights / jnp.sum(weights, axis=-1, keepdims=True)).astype(jnp.bfloat16)
    mixed = jnp.einsum("rhqp,rpd->rqhd", probs, value_blocks, preferred_element_type=jnp.float32)
    live = slot_pos[None, :] < request_token_length[:, None]
    mixed = jnp.where(live[:, :, None, None], mixed, jnp.float32(0.0))
    return mixed.astype(jnp.bfloat16).reshape(tok_rows, query_cols)


def solution(mesh):
    placed = (
        P("rep", "tp"),
        P(None, "tp"),
        P("tp", None),
        P("rep", None, "tp"),
        P("rep", None, "tp"),
        P("rep", None, "tp"),
        P("rep"),
        P("rep"),
        P(),
    )
    return jax.shard_map(
        shards, mesh=mesh, in_specs=placed, out_specs=P("rep", "tp"), check_vma=False
    )
```

profile of v0, /device:TPU:0, one launch (start us, length us, event | category | flops | bytes accessed | tf_op | source)
XLA Modules:
  0.0 532.3 jit_solution(14135804955367768476)
XLA Ops:
  7.9 9.6 %all_to_all.30 = s32[8,1,4]{2,1,0:T(1,128)S(1)} all-to-all(s32[8,1,4]{2,1,0:T(1,128)S(1)} %bitcast.83), channel_id=1, replica_groups=mesh['rep'=8,'tp'=4] {'rep'}, dimensions={0} | all-to-all | bytes 256 | tf_op jit(solution)/shard_map/all_to_all | solution.py:100
  17.9 9.9 %gather_fusion = bf16[32,192,2048]{2,1,0:T(8,128)(2,1)} fusion(bf16[4,192,2048]{2,1,0:T(8,128)(2,1)S(1)} %copy-done, s32[1024]{0:T(1024)S(1)} %pad_clamp_fusion), kind=kCustom, calls=%fused_computation | custom fusion | bytes 50331776 | tf_op jit(solution)/shard_map/jit(_take)/gather | solution.py:103
  29.6 3.6 all-to-all-start.3
  33.2 21.2 %broadcast_select_fusion = bf16[8,4,192,2048]{3,2,1,0:T(8,128)(2,1)} fusion(bf16[8,4,192,2048]{3,2,1,0:T(8,128)(2,1)} %bitcast.69, pred[8,4]{1,0:T(8,128)(4,1)S(1)} %copy.40), kind=kLoop, calls=%fused_computation.5 | loop fusion | flops 12582912 | bytes 50331680 | tf_op jit(solution)/shard_map/jit(_take)/select_n | solution.py:103
  55.3 6.4 %all-to-all-start.1 = ((bf16[8,4,192,2048]{3,2,1,0:T(8,128)(2,1)}), bf16[8,4,192,2048]{3,2,1,0:T(8,128)(2,1)}, u32[]{:S(2)}, u32[]{:S(2)}) async-start(bf16[8,4,192,2048]{3,2,1,0:T(8,128)(2,1)} %broadcast_select_fusion), calls=%async_computation.1 | async-start | bytes 50331648 | tf_op jit(solution)/shard_map/all_to_all | solution.py:102
  62.5 2.2 reshape.310
  64.8 3.3 convolution_convert_fusion
  68.1 2.8 gather_fusion.1
  70.9 5.1 broadcast_select_fusion.1
  76.0 259.6 %all-to-all-done.1 = bf16[8,4,192,2048]{3,2,1,0:T(8,128)(2,1)} async-done(((bf16[8,4,192,2048]{3,2,1,0:T(8,128)(2,1)}), bf16[8,4,192,2048]{3,2,1,0:T(8,128)(2,1)}, u32[]{:S(2)}, u32[]{:S(2)}) %all-to-all-start.1) | async-done | bytes 25165856 | tf_op jit(solution)/shard_map/all_to_all | solution.py:102
  335.6 4.8 all-to-all-start.2
  340.4 6.6 %copy.52 = bf16[4,8,32,2048]{3,2,1,0:T(8,128)(2,1)} copy(bf16[4,8,32,2048]{3,1,2,0:T(8,128)(2,1)} %bitcast.71) | data formatting | bytes 8388608
  349.5 5.8 %fusion.48 = f32[512,1024]{1,0:T(8,128)} fusion(bf16[512,2048]{1,0:T(8,128)(2,1)S(1)} %copy-done.3, bf16[2048,1024]{1,0:T(8,128)(2,1)} %param.11), kind=kOutput, calls=%fused_computation.86 | convolution fusion | flops 2147483648 | bytes 8388608 | tf_op jit(solution)/shard_map/dot_general | solution.py:79
  355.4 13.4 %fusion.49 = f32[8,4,32,192]{3,2,1,0:T(8,128)S(1)} fusion(bf16[8,4,32,2048]{3,2,1,0:T(8,128)(2,1)} %bitcast.73, bf16[8,4,192,2048]{3,2,1,0:T(8,128)(2,1)} %all-to-all-done.1), kind=kOutput, calls=%fused_computation.87 | convolution fusion | flops 805306368 | bytes 30146560 | tf_op jit(solution)/shard_map/scnf,scrf->scnr/dot_general | solution.py:124
  368.8 43.8 %all-reduce.2 = bf16[8,4,32,192]{3,2,1,0:T(8,128)(2,1)S(1)} all-reduce(f32[8,4,32,192]{3,2,1,0:T(8,128)S(1)} %fusion.49), channel_id=1, replica_groups=mesh['rep'=8,'tp'=4] {'tp'}, use_global_device_ids=true, to_apply=%region_3.4 | all-reduce | flops 196608 | bytes 1179648 | tf_op jit(solution)/shard_map/psum | solution.py:127
  413.0 2.9 fusion.23
  418.1 2.1 fusion.32
  420.1 1.9 reshape.312
  422.1 2.0 fusion.12
  424.0 72.7 %all-reduce.3 = bf16[512,1024]{1,0:T(8,128)(2,1)} all-reduce(f32[512,1024]{1,0:T(8,128)} %fusion.12), channel_id=1, replica_groups=mesh['rep'=8,'tp'=4] {'tp'}, use_global_device_ids=true, to_apply=%region_4.5 | all-reduce | flops 524288 | bytes 3145728 | tf_op jit(solution)/shard_map/psum | solution.py:146
  497.7 1.9 fusion.18
  499.6 14.4 %fusion.2 = f32[64,8,8,128]{3,1,2,0:T(8,128)S(1)} fusion(f32[512,1280]{1,0:T(8,128)S(1)} %reshape.312, bf16[512,8192]{1,0:T(8,128)(2,1)} %all-gather.2.cloned.1.call-done, bf16[8192,1024]{1,0:T(8,128)(2,1)} %param.10), kind=kOutput, calls=%fused_computation.10 | convolution fusion | flops 8590458880 | bytes 29360128 | tf_op jit(solution)/shard_map/dot_general | solution.py:74
  516.7 4.7 fusion.45
  521.4 2.3 fusion.4
  (58 shorter events, 15.7 us)
Async XLA Ops:
  6.5 11.4 %copy-start = (bf16[4,192,2048]{2,1,0:T(8,128)(2,1)S(1)}, bf16[4,192,2048]{2,1,0:T(8,128)(2,1)}, u32[]{:S(2)}) copy-start(bf16[4,192,2048]{2,1,0:T(8,128)(2,1)} %param.12) | copy-start | bytes 9437188
  17.9 9.9 %copy-start.4 = (bf16[4,64,256]{2,1,0:T(8,128)(2,1)S(1)}, bf16[4,64,256]{2,1,0:T(8,128)(2,1)}, u32[]{:S(2)}) copy-start(bf16[4,64,256]{2,1,0:T(8,128)(2,1)} %param.14) | copy-start | bytes 393220
  29.6 24.8 %all-to-all-start.3 = ((bf16[8,4,64,256]{3,2,1,0:T(8,128)(2,1)}), bf16[8,4,64,256]{3,2,1,0:T(8,128)(2,1)S(1)}, u32[]{:S(2)}, u32[]{:S(2)}) async-start(bf16[8,4,64,256]{3,2,1,0:T(8,128)(2,1)} %broadcast_select_fusion.2), calls=%async_computation.3 | async-start | bytes 2097152 | tf_op jit(solution)/shard_map/all_to_all | solution.py:116
  54.4 1.0 copy-start.5
  55.3 280.3 %all-to-all-start.1 = ((bf16[8,4,192,2048]{3,2,1,0:T(8,128)(2,1)}), bf16[8,4,192,2048]{3,2,1,0:T(8,128)(2,1)}, u32[]{:S(2)}, u32[]{:S(2)}) async-start(bf16[8,4,192,2048]{3,2,1,0:T(8,128)(2,1)} %broadcast_select_fusion), calls=%async_computation.1 | async-start | bytes 50331648 | tf_op jit(solution)/shard_map/all_to_all | solution.py:102
  61.8 437.8 %all-gather.2.cloned.1.call-start = ((), (), s32[]{:S(2)}) async-start(), calls=%async_computation.4 | async-start | bytes 10485760 | tf_op jit(solution)/shard_map/all_gather | solution.py:75
  62.5 2.3 copy-start.10
  64.8 3.3 copy-start.2
  335.6 77.4 %all-to-all-start.2 = ((bf16[8,4,64,1024]{3,2,1,0:T(8,128)(2,1)}), bf16[8,4,64,1024]{3,2,1,0:T(8,128)(2,1)}, u32[]{:S(2)}, u32[]{:S(2)}) async-start(bf16[8,4,64,1024]{3,2,1,0:T(8,128)(2,1)} %broadcast_select_fusion.1), calls=%async_computation.2 | async-start | bytes 8388608 | tf_op jit(solution)/shard_map/all_to_all | solution.py:109
  340.4 9.1 %copy-start.3 = (bf16[512,2048]{1,0:T(8,128)(2,1)S(1)}, bf16[512,2048]{1,0:T(8,128)(2,1)}, u32[]{:S(2)}) copy-start(bf16[512,2048]{1,0:T(8,128)(2,1)} %param.9) | copy-start | bytes 6291460
  355.4 57.3 %copy-start.6 = (bf16[8,4,64,256]{3,2,1,0:T(8,128)(2,1)S(1)}, bf16[8,4,64,256]{3,2,1,0:T(8,128)(2,1)}, u32[]{:S(2)}) copy-start(bf16[8,4,64,256]{3,2,1,0:T(8,128)(2,1)} %copy-done.5) | copy-start | bytes 3145732
  513.9 1.0 copy-start.7
  515.7 0.9 copy-start.8
  515.7 1.0 copy-start.9
  521.4 4.0 copy-start.1
Sparse Core Ops, SparseCore 0:
  64.2 151.2 all-gather.1
where the time goes:
time: 533 us; the launch traced here: 532 us
  waiting for transfers between devices  260 us (49%)
  blocking collectives  126 us (24%)
  matrix products  49.3 us (9%)
  other arithmetic  37.6 us (7%)
  local copies, waits for them, and re-layouts  30.5 us (6%)
  starting transfers between devices  14.8 us (3%)
  between operations  13.6 us (3%)
    all_to_all x1, waiting for transfers between devices, shards(): lax.all_to_all(jnp.take(adapter_down_tables, needed_locally, axis=0), 're...  260 us
    psum x1, blocking collectives, shards(): pair_full = lax.psum(base_pair + placed, 'tp')  72.7 us
    psum x1, blocking collectives, shards(): shrink = lax.psum(partial_sum, 'tp').astype(jnp.bfloat16)  43.8 us
    select_n x2, other arithmetic, shards(): jnp.take(adapter_down_tables, needed_locally, axis=0)  21.2 us
    dot_general x1, matrix products, shards(): jnp.dot(lax.all_gather(tokens, 'tp', axis=1, tiled=True), query_weight, p...  14.4 us
    dot_general x1, matrix products, shards(): jnp.einsum('scnf,scrf->scnr', send_rows, fetched_down, preferred_element_...  13.4 us
    unnamed x26, local copies, waits for them, and re-layouts  11.7 us
  transfers between devices with their start and end apart: 4, of which 1 were waited for; matrix products, arithmetic and copies ran while one was open for 15% of the time, Pallas kernels for 0%

commit v1 on v0

--- a/solution.py
+++ b/solution.py
@@ -7,6 +7,12 @@
 HEAD_SIZE = 128
 adapter_scale = 0.5
 rope_theta = 500000.0
+
+
+def gather_and_add(value, name):
+    pieces = lax.all_gather(value, name, axis=0, tiled=False)
+    total = pieces.sum(axis=0)
+    return total
 
 
 def rotary(values, positions):
@@ -124,7 +130,7 @@
     partial_sum = jnp.einsum(
         "scnf,scrf->scnr", send_rows, fetched_down, preferred_element_type=jnp.float32
     )
-    shrink = lax.psum(partial_sum, "tp").astype(jnp.bfloat16)
+    shrink = gather_and_add(partial_sum, "tp").astype(jnp.bfloat16)
     returned = expand_slots(shrink, fetched_query, fetched_pair, value_side)
     delta = jnp.dot(
         place_matrix.T,

time: 533 us -> 675 us (1.27)
  waiting for transfers between devices: 260 us -> 372 us
  blocking collectives: 126 us -> 157 us
    psum x1, blocking collectives: 72.7 us -> 147 us  [shards(): pair_full = lax.psum(base_pair + placed, 'tp')]
    all_gather x1, waiting for transfers between devices: 0.01 us -> 52.3 us  [shards(): lax.all_gather(tokens, 'tp', axis=1, tiled=True)]
    all_gather x0 -> x1, waiting for transfers between devices: none -> 45.6 us  [gather_and_add(): pieces = lax.all_gather(value, name, axis=0, tiled=False)]
    psum x1 -> x0, blocking collectives: 43.8 us -> none  [shards(): shrink = lax.psum(partial_sum, 'tp').astype(jnp.bfloat16)]
    all_to_all x1, waiting for transfers between devices: 0.01 us -> 7.81 us  [shards(): lax.all_to_all(jnp.take(adapter_up_key_value, needed_locally, axis=0), 'r...]
  transfers between devices with their start and end apart: 4 -> 5, of which waited for: 1 -> 4; matrix products, arithmetic and copies ran while one was open for 15% -> 6% of each run, Pallas kernels for 0% -> 0%
where the time goes in v1:
time: 675 us; the launch traced here: 674 us
  waiting for transfers between devices  372 us (55%)
  blocking collectives  157 us (23%)
  matrix products  48.4 us (7%)
  other arithmetic  40.1 us (6%)
  local copies, waits for them, and re-layouts  27.5 us (4%)
  starting transfers between devices  14.8 us (2%)
  between operations  13.6 us (2%)
    all_to_all x1, waiting for transfers between devices, shards(): lax.all_to_all(jnp.take(adapter_down_tables, needed_locally, axis=0), 're...  266 us
    psum x1, blocking collectives, shards(): pair_full = lax.psum(base_pair + placed, 'tp')  147 us
    all_gather x1, waiting for transfers between devices, shards(): lax.all_gather(tokens, 'tp', axis=1, tiled=True)  52.3 us
    all_gather x1, waiting for transfers between devices, gather_and_add(): pieces = lax.all_gather(value, name, axis=0, tiled=False)  45.6 us
    select_n x2, other arithmetic, shards(): jnp.take(adapter_down_tables, needed_locally, axis=0)  21.2 us
    dot_general x1, matrix products, shards(): jnp.einsum('scnf,scrf->scnr', send_rows, fetched_down, preferred_element_...  14.4 us
    dot_general x1, matrix products, shards(): jnp.dot(lax.all_gather(tokens, 'tp', axis=1, tiled=True), query_weight, p...  14.4 us
  transfers between devices with their start and end apart: 5, of which 4 were waited for; matrix products, arithmetic and copies ran while one was open for 6% of the time, Pallas kernels for 0%

profile of v1, /device:TPU:0, one launch (start us, length us, event | category | flops | bytes accessed | tf_op | source)
XLA Modules:
  0.0 673.7 jit_solution(2643766776227555749)
XLA Ops:
  7.9 9.6 %all_to_all.30 = s32[8,1,4]{2,1,0:T(1,128)S(1)} all-to-all(s32[8,1,4]{2,1,0:T(1,128)S(1)} %bitcast.85), channel_id=1, replica_groups=mesh['rep'=8,'tp'=4] {'rep'}, dimensions={0} | all-to-all | bytes 256 | tf_op jit(solution)/shard_map/all_to_all | solution.py:106
  17.9 9.9 %gather_fusion = bf16[32,192,2048]{2,1,0:T(8,128)(2,1)} fusion(bf16[4,192,2048]{2,1,0:T(8,128)(2,1)S(1)} %copy-done, s32[1024]{0:T(1024)S(1)} %pad_clamp_fusion), kind=kCustom, calls=%fused_computation | custom fusion | bytes 50331776 | tf_op jit(solution)/shard_map/jit(_take)/gather | solution.py:109
  27.8 21.2 %broadcast_select_fusion = bf16[8,4,192,2048]{3,2,1,0:T(8,128)(2,1)} fusion(bf16[8,4,192,2048]{3,2,1,0:T(8,128)(2,1)} %bitcast.70, pred[8,4]{1,0:T(8,128)(4,1)S(1)} %copy.40), kind=kLoop, calls=%fused_computation.5 | loop fusion | flops 12582912 | bytes 50331680 | tf_op jit(solution)/shard_map/jit(_take)/select_n | solution.py:109
  49.0 6.4 all-to-all-start.1
  55.5 2.2 reshape.310
  59.1 4.3 copy.52
  63.4 265.9 %all-to-all-done.1 = bf16[8,4,192,2048]{3,2,1,0:T(8,128)(2,1)} async-done(((bf16[8,4,192,2048]{3,2,1,0:T(8,128)(2,1)}), bf16[8,4,192,2048]{3,2,1,0:T(8,128)(2,1)}, u32[]{:S(2)}, u32[]{:S(2)}) %all-to-all-start.1) | async-done | bytes 25165856 | tf_op jit(solution)/shard_map/all_to_all | solution.py:108
  329.3 14.4 %fusion.49 = f32[8,4,32,192]{3,2,1,0:T(8,128)} fusion(bf16[8,4,32,2048]{3,2,1,0:T(8,128)(2,1)} %bitcast.74, bf16[8,4,192,2048]{3,2,1,0:T(8,128)(2,1)} %all-to-all-done.1), kind=kOutput, calls=%fused_computation.87 | convolution fusion | flops 805306368 | bytes 30146560 | tf_op jit(solution)/shard_map/scnf,scrf->scnr/dot_general | solution.py:130
  346.4 3.6 all-to-all-start.3
  350.0 2.8 gather_fusion.1
  352.7 4.8 broadcast_select_fusion.1
  357.5 7.8 %all-to-all-done.3 = bf16[8,4,64,256]{3,2,1,0:T(8,128)(2,1)S(1)} async-done(((bf16[8,4,64,256]{3,2,1,0:T(8,128)(2,1)}), bf16[8,4,64,256]{3,2,1,0:T(8,128)(2,1)S(1)}, u32[]{:S(2)}, u32[]{:S(2)}) %all-to-all-start.3) | async-done | bytes 1048608 | tf_op jit(solution)/shard_map/all_to_all | solution.py:122
  365.3 4.7 all-to-all-start.2
  372.7 5.8 fusion.48
  378.5 45.6 %all-gather.6.cloned.1.call-done = f32[32,4,32,192]{3,2,1,0:T(8,128)} async-done(((f32[8,4,32,192]{3,2,1,0:T(8,128)}), f32[32,4,32,192]{3,2,1,0:T(8,128)}) %all-gather.6.cloned.1.call-update) | async-done | bytes 3145744 | tf_op jit(solution)/shard_map/all_gather | solution.py:13
  424.1 2.8 reduce_sum.48
  427.2 2.9 fusion.23
  432.3 2.1 fusion.32
  434.4 2.1 reshape.312
  438.5 147.3 %all-reduce.1 = bf16[512,1024]{1,0:T(8,128)(2,1)} all-reduce(f32[512,1024]{1,0:T(8,128)} %fusion.12), channel_id=1, replica_groups=mesh['rep'=8,'tp'=4] {'tp'}, use_global_device_ids=true, to_apply=%region_4.5 | all-reduce | flops 524288 | bytes 3145728 | tf_op jit(solution)/shard_map/psum | solution.py:152
  588.7 52.3 %all-gather.4.cloned.1.call-done = bf16[512,8192]{1,0:T(8,128)(2,1)} async-done(((bf16[512,2048]{1,0:T(8,128)(2,1)}), bf16[512,8192]{1,0:T(8,128)(2,1)}) %all-gather.4.cloned.1.call-update) | async-done | bytes 8388624 | tf_op jit(solution)/shard_map/all_gather | solution.py:81
  641.0 14.4 %fusion.2 = f32[64,8,8,128]{3,1,2,0:T(8,128)S(1)} fusion(f32[512,1280]{1,0:T(8,128)S(1)} %reshape.312, bf16[512,8192]{1,0:T(8,128)(2,1)} %all-gather.4.cloned.1.call-done, bf16[8192,1024]{1,0:T(8,128)(2,1)} %param.10), kind=kOutput, calls=%fused_computation.10 | convolution fusion | flops 8590458880 | bytes 29360128 | tf_op jit(solution)/shard_map/dot_general | solution.py:80
  658.1 4.7 fusion.45
  662.8 2.3 fusion.4
  (57 shorter events, 20.1 us)
Async XLA Ops:
  6.5 11.4 %copy-start = (bf16[4,192,2048]{2,1,0:T(8,128)(2,1)S(1)}, bf16[4,192,2048]{2,1,0:T(8,128)(2,1)}, u32[]{:S(2)}) copy-start(bf16[4,192,2048]{2,1,0:T(8,128)(2,1)} %param.12) | copy-start | bytes 9437188
  49.0 280.3 %all-to-all-start.1 = ((bf16[8,4,192,2048]{3,2,1,0:T(8,128)(2,1)}), bf16[8,4,192,2048]{3,2,1,0:T(8,128)(2,1)}, u32[]{:S(2)}, u32[]{:S(2)}) async-start(bf16[8,4,192,2048]{3,2,1,0:T(8,128)(2,1)} %broadcast_select_fusion), calls=%async_computation.1 | async-start | bytes 50331648 | tf_op jit(solution)/shard_map/all_to_all | solution.py:108
  55.5 368.6 %all-gather.6.cloned.1.call-start = ((), (), s32[]{:S(2)}) async-start(), calls=%async_computation.5 | async-start | bytes 5242880 | tf_op jit(solution)/shard_map/all_gather | solution.py:13
  343.7 0.9 copy-start.4
  343.8 297.2 %all-gather.4.cloned.1.call-start = ((), (), s32[]{:S(2)}) async-start(), calls=%async_computation.4 | async-start | bytes 10485760 | tf_op jit(solution)/shard_map/all_gather | solution.py:81
  345.3 4.7 copy-start.2
  346.4 18.9 %all-to-all-start.3 = ((bf16[8,4,64,256]{3,2,1,0:T(8,128)(2,1)}), bf16[8,4,64,256]{3,2,1,0:T(8,128)(2,1)S(1)}, u32[]{:S(2)}, u32[]{:S(2)}) async-start(bf16[8,4,64,256]{3,2,1,0:T(8,128)(2,1)} %broadcast_select_fusion.2), calls=%async_computation.3 | async-start | bytes 2097152 | tf_op jit(solution)/shard_map/all_to_all | solution.py:122
  357.5 12.6 %copy-start.8 = (s32[16]{0:T(128)S(1)}, s32[16]{0:T(128)}, u32[]{:S(2)}) copy-start(s32[16]{0:T(128)} %param.16) | copy-start | bytes 196
  357.5 15.2 %copy-start.3 = (bf16[512,2048]{1,0:T(8,128)(2,1)S(1)}, bf16[512,2048]{1,0:T(8,128)(2,1)}, u32[]{:S(2)}) copy-start(bf16[512,2048]{1,0:T(8,128)(2,1)} %param.9) | copy-start | bytes 6291460
  365.3 61.9 %all-to-all-start.2 = ((bf16[8,4,64,1024]{3,2,1,0:T(8,128)(2,1)}), bf16[8,4,64,1024]{3,2,1,0:T(8,128)(2,1)}, u32[]{:S(2)}, u32[]{:S(2)}) async-start(bf16[8,4,64,1024]{3,2,1,0:T(8,128)(2,1)} %broadcast_select_fusion.1), calls=%async_computation.2 | async-start | bytes 8388608 | tf_op jit(solution)/shard_map/all_to_all | solution.py:115
  655.3 1.0 copy-start.5
  657.1 0.9 copy-start.6
  657.1 1.0 copy-start.7
  662.8 4.0 copy-start.1
Sparse Core Ops, SparseCore 0:
  343.9 80.1 all-gather.5
  425.6 215.2 all-gather.3
